TPU v7x, 512 devices: a whole 4x4x16 slice. The times are simulated.
512 devices in a mesh: blk: 16 (over y_lo, x, core), grp: 32 (over z, y_hi).
Axes of the slice: x: 4, y: 4 (y_hi: 2, y_lo: 2; y = y_hi * 2 + y_lo), z: 16, core: 2. Of those that a mesh axis runs over, the one named last changes fastest.
Arguments:
- amps: bfloat16 [4096, 8, 512], P(('blk', 'grp')), may hold values from -6 to 6
- domains: int32 [4096, 8], replicated, may hold values from 0 to 15, all different within a row
- owner: int32 [4096], replicated, may hold values from 0 to 4095, as said below
- coupling: int32 [16, 16], replicated, may hold values from 0 to 1, as said below
- integrals: bfloat16 [8192, 8192], P('blk', 'grp'), may hold values from -0.125 to 0.125
Outputs:
- residual: float32 [4096, 8192], P('blk', 'grp')
Inputs may be any that keep to these rules, and one draw needn't show every extreme that they name: `domains`: each row names 8 different pair blocks, and every block is named by some row. owner maps the occupied pairs of each group of 256 consecutive pairs one to one onto the slots of the same group. Every column of coupling holds exactly 8 ones.
All inputs are finite; a program needn't handle non-finite values.
Results may differ from a plain program's by a relative error of at most 0.0003.
Values may be sent and summed in bfloat16 or wider, within the bound.
No kernel may reach another device: no remote copies, remote signals or barrier semaphores. Data moves between devices by JAX's collectives and lax.ppermute only.
A program may use at most 64 MiB of HBM per device.

v0:
```python
import jax
import jax.numpy as jnp
from jax import lax
from jax.sharding import PartitionSpec as P


def on_device(amps, domains, owner, coupling, integrals):
    n_blk = lax.axis_size("blk")
    me_blk = lax.axis_index("blk")
    me_grp = lax.axis_index("grp")
    block_rows, col_count = integrals.shape
    col_split = block_rows // col_count
    nvb = coupling.shape[0]
    op_total = owner.shape[0]
    op_grp = op_total // n_blk
    dom_width = domains.shape[1]
    target = me_grp // col_split
    blocks = jnp.arange(nvb, dtype=jnp.int32)
    keep_col = lax.dynamic_index_in_dim(coupling, target, axis=1, keepdims=False)
    group_base = me_blk * op_grp
    own_pairs = lax.dynamic_slice_in_dim(owner, group_base, op_grp)
    local_slots = own_pairs - group_base
    group_dom = lax.dynamic_slice_in_dim(domains, group_base, op_grp)
    permuter = (local_slots[:, None] == jnp.arange(op_grp, dtype=jnp.int32)[None, :]).astype(
        jnp.float32
    )
    pair_dom = jnp.dot(
        permuter, group_dom.astype(jnp.float32), precision=lax.Precision.HIGHEST
    ).astype(jnp.int32)
    in_domain = jnp.any(pair_dom == target, axis=1).astype(jnp.float32)
    group_amps = lax.all_gather(amps, "grp", axis=0, tiled=True)
    flat_amps = group_amps.reshape(op_grp, dom_width * block_rows)
    ordered = jnp.take(flat_amps, local_slots, axis=0).reshape(op_grp, dom_width, block_rows)
    selector = (pair_dom[:, :, None] == blocks[None, None, :]) & (keep_col[None, None, :] > 0)
    tile_full = jnp.einsum(
        "pkc,pkx->pcx", selector.astype(jnp.bfloat16), ordered, preferred_element_type=jnp.float32
    )
    tile_full = tile_full.astype(jnp.bfloat16).reshape(op_grp, nvb * block_rows)
    summed = jnp.dot(
        tile_full,
        lax.all_gather(integrals, "blk", axis=0, tiled=True),
        preferred_element_type=jnp.float32,
    )
    return summed * in_domain[:, None]


def solution(mesh):
    return jax.shard_map(
        on_device,
        mesh=mesh,
        in_specs=(P(("blk", "grp"), None, None), P(), P(), P(), P("blk", "grp")),
        out_specs=P("blk", "grp"),
        check_vma=False,
    )
```

profile of v0, /device:TPU:1, one launch (start us, length us, event | category | flops | bytes accessed | tf_op | source)
XLA Modules:
  0.0 219.4 jit_solution(15730783104113241704)
XLA Ops:
  6.5 0.0 all-gather.3.cloned.1.call-start
  6.5 0.7 all-gather.3.cloned.1.call-update
  7.3 0.0 all-gather.5.cloned.1.call-start
  7.3 0.7 all-gather.5.cloned.1.call-update
  8.0 0.8 compare_and_fusion
  8.8 1.0 compare_reduce_fusion
  9.8 0.1 copy.8
  10.0 0.9 fusion.7
  10.9 145.2 %all-gather.3.cloned.1.call-done = bf16[256,8,512]{2,1,0:T(8,128)(2,1)} async-done(((bf16[8,8,512]{2,1,0:T(8,128)(2,1)}), bf16[256,8,512]{2,1,0:T(8,128)(2,1)}) %all-gather.3.cloned.1.call-update) | async-done | bytes 2097168 | tf_op jit(solution)/shard_map/all_gather | solution.py:31
  156.1 2.5 %copy.9 = bf16[32,8,8,512]{3,1,2,0:T(8,128)(2,1)S(1)} copy(bf16[32,8,8,512]{3,2,1,0:T(8,128)(2,1)} %bitcast.14) | data formatting | bytes 4194304
  158.6 3.2 %gather_fusion = bf16[256,4096]{1,0:T(8,128)(2,1)} fusion(bf16[256,4096]{1,0:T(8,128)(2,1)S(1)} %bitcast.10, s32[1024]{0:T(1024)S(1)} %pad_clamp_fusion), kind=kCustom, calls=%fused_computation | custom fusion | bytes 4195328 | tf_op jit(solution)/shard_map/jit(_take)/gather | solution.py:33
  161.7 2.5 %copy.10 = bf16[32,8,8,512]{3,2,1,0:T(8,128)(2,1)S(1)} copy(bf16[32,8,8,512]{3,1,2,0:T(8,128)(2,1)} %bitcast.12) | data formatting | bytes 4194304
  164.2 1.1 bitcast_select_fusion
  165.3 3.7 %convolution_convert_fusion = bf16[256,16,512]{2,1,0:T(8,128)(2,1)S(1)} fusion(bf16[256,8,512]{2,1,0:T(8,128)(2,1)S(1)} %bitcast_select_fusion, s32[256,8]{1,0:T(8,128)S(1)} %copy.8, pred[16]{0:T(512)(128)(4,1)S(1)} %fusion.7), kind=kOutput, calls=%fused_computation.1 | convolution fusion | flops 35717120 | bytes 6299664 | tf_op jit(solution)/shard_map/pkc,pkx->pcx/dot_general | solution.py:35
  169.1 6.3 %copy.11 = bf16[32,8,16,512]{3,1,2,0:T(8,128)(2,1)} copy(bf16[32,8,16,512]{3,2,1,0:T(8,128)(2,1)S(1)} %bitcast.11) | data formatting | bytes 8388608
  175.3 31.8 %all-gather.5.cloned.1.call-done = bf16[8192,256]{1,0:T(8,128)(2,1)} async-done(((bf16[512,256]{1,0:T(8,128)(2,1)}), bf16[8192,256]{1,0:T(8,128)(2,1)}) %all-gather.5.cloned.1.call-update) | async-done | bytes 4194320 | tf_op jit(solution)/shard_map/all_gather | solution.py:41
  207.1 5.4 %convolution_multiply_fusion = f32[256,256]{1,0:T(8,128)} fusion(bf16[256,8192]{1,0:T(8,128)(2,1)} %bitcast.13, bf16[8192,256]{1,0:T(8,128)(2,1)} %all-gather.5.cloned.1.call-done, f32[256]{0:T(256)S(1)} %convert_element_type.21), kind=kOutput, calls=%fused_computation.3 | convolution fusion | flops 1073807360 | bytes 8651776 | tf_op jit(solution)/shard_map/dot_general | solution.py:39
  (3 shorter events, 0.0 us)
Async XLA Ops:
  6.5 149.5 %all-gather.3.cloned.1.call-start = ((), (), s32[]{:S(2)}) async-start(), calls=%async_computation | async-start | bytes 2162688 | tf_op jit(solution)/shard_map/all_gather | solution.py:31
  7.3 199.9 %all-gather.5.cloned.1.call-start = ((), (), s32[]{:S(2)}) async-start(), calls=%async_computation.1 | async-start | bytes 4456448 | tf_op jit(solution)/shard_map/all_gather | solution.py:41
Sparse Core Ops, SparseCore 0:
  10.4 145.5 all-gather.2
  158.2 48.8 all-gather.4
where the time goes:
time: 220 us; the launch traced here: 219 us
  waiting for transfers between devices  178 us (81%)
  local copies, waits for them, and re-layouts  14.5 us (7%)
  between operations  13.5 us (6%)
  matrix products  10.2 us (5%)
  other arithmetic  2.75 us (1%)
    all_gather x1, waiting for transfers between devices, on_device(): group_amps = lax.all_gather(amps, 'grp', axis=0, tiled=True)  145 us
    all_gather x1, waiting for transfers between devices, on_device(): lax.all_gather(integrals, 'blk', axis=0, tiled=True)  31.8 us
    unnamed x3, local copies, waits for them, and re-layouts  11.2 us
    dot_general x1, matrix products, on_device(): jnp.dot(tile_full, lax.all_gather(integrals, 'blk', axis=0, tiled=True),...  5.42 us
  transfers between devices with their start and end apart: 2, of which 2 were waited for; matrix products, arithmetic and copies ran while one was open for 10% of the time, Pallas kernels for 0%

commit v1 on v0

--- a/solution.py
+++ b/solution.py
@@ -2,6 +2,7 @@
 import jax.numpy as jnp
 from jax import lax
 from jax.sharding import PartitionSpec as P
+from jax.lax import all_to_all, psum
 
 
 def on_device(amps, domains, owner, coupling, integrals):
@@ -38,7 +39,9 @@
     tile_full = tile_full.astype(jnp.bfloat16).reshape(op_grp, nvb * block_rows)
     summed = jnp.dot(
         tile_full,
-        lax.all_gather(integrals, "blk", axis=0, tiled=True),
+        jnp.concatenate(
+            all_to_all(jnp.stack(psum(1, "blk") * [integrals], axis=0), "blk", 0, 0), 0
+        ),
         preferred_element_type=jnp.float32,
     )
     return summed * in_domain[:, None]

time: 220 us -> 205 us (0.932)
  the two profiles are of different devices: /device:TPU:1 before, /device:TPU:2 now
where the time goes in v1:
time: 205 us
  waiting for transfers between devices  153 us (75%)
  matrix products  14.9 us (7%)
  between operations  13.4 us (7%)
  local copies, waits for them, and re-layouts  11.6 us (6%)
  starting transfers between devices  10.3 us (5%)
  other arithmetic  2.06 us (1%)
    all_gather x1, waiting for transfers between devices, on_device(): group_amps = lax.all_gather(amps, 'grp', axis=0, tiled=True)  152 us
    all_to_all x1, starting transfers between devices, on_device(): all_to_all(jnp.stack(psum(1, 'blk') * [integrals], axis=0), 'blk', 0, 0)  10.3 us
    dot_general x1, matrix products, on_device(): jnp.dot(tile_full, jnp.concatenate(all_to_all(jnp.stack(psum(1, 'blk') *...  8.87 us
    dot_general x1, matrix products, on_device(): jnp.einsum('pkc,pkx->pcx', selector.astype(jnp.bfloat16), ordered, prefer...  5.04 us
    unnamed x4, local copies, waits for them, and re-layouts  4.97 us
  transfers between devices with their start and end apart: 2, of which 1 were waited for; matrix products, arithmetic and copies ran while one was open for 10% of the time, Pallas kernels for 0%

profile of v1, /device:TPU:2, one launch (start us, length us, event | category | flops | bytes accessed | tf_op | source)
XLA Modules:
  0.0 205.0 jit_solution(12593773195904983348)
XLA Ops:
  6.5 0.0 all-gather.2.cloned.1.call-start
  6.5 0.7 all-gather.2.cloned.1.call-update
  7.3 3.3 %stack.2 = bf16[16,512,256]{2,1,0:T(8,128)(2,1)} broadcast(bf16[512,256]{1,0:T(8,128)(2,1)} %param.9), dimensions={1,2} | broadcast | bytes 4456448 | tf_op jit(solution)/shard_map/stack | solution.py:43
  10.6 0.0 copy-start
  10.6 10.3 %all-to-all-start = ((bf16[16,512,256]{2,1,0:T(8,128)(2,1)}), bf16[16,512,256]{2,1,0:T(8,128)(2,1)}, u32[]{:S(2)}, u32[]{:S(2)}) async-start(bf16[16,512,256]{2,1,0:T(8,128)(2,1)} %stack.2), calls=%async_computation | async-start | bytes 8388608 | tf_op jit(solution)/shard_map/all_to_all | solution.py:43
  20.9 0.8 compare_and_fusion
  21.6 1.0 compare_reduce_fusion
  22.7 0.1 copy.8
  22.8 0.0 copy-done
  22.8 0.2 fusion.15
  23.0 151.9 %all-gather.2.cloned.1.call-done = bf16[256,8,512]{2,1,0:T(8,128)(2,1)} async-done(((bf16[8,8,512]{2,1,0:T(8,128)(2,1)}), bf16[256,8,512]{2,1,0:T(8,128)(2,1)}) %all-gather.2.cloned.1.call-update) | async-done | bytes 2097168 | tf_op jit(solution)/shard_map/all_gather | solution.py:32
  174.9 2.5 %copy.10 = bf16[32,8,8,512]{3,1,2,0:T(8,128)(2,1)S(1)} copy(bf16[32,8,8,512]{3,2,1,0:T(8,128)(2,1)} %bitcast.13) | data formatting | bytes 4194304
  177.4 3.2 %gather_fusion = bf16[256,4096]{1,0:T(8,128)(2,1)} fusion(bf16[256,4096]{1,0:T(8,128)(2,1)S(1)} %bitcast.11, s32[1024]{0:T(1024)S(1)} %pad_clamp_fusion), kind=kCustom, calls=%fused_computation | custom fusion | bytes 4195328 | tf_op jit(solution)/shard_map/jit(_take)/gather | solution.py:34
  180.6 2.5 %copy.11 = bf16[32,8,8,512]{3,2,1,0:T(8,128)(2,1)S(1)} copy(bf16[32,8,8,512]{3,1,2,0:T(8,128)(2,1)} %bitcast.12) | data formatting | bytes 4194304
  183.1 1.1 bitcast_select_fusion
  184.2 5.0 %convolution_convert_fusion = bf16[256,16,512]{2,1,0:T(8,128)(2,1)} fusion(bf16[256,8,512]{2,1,0:T(8,128)(2,1)S(1)} %bitcast_select_fusion, s32[256,8]{1,0:T(8,128)S(1)} %copy.8, pred[16]{0:T(512)(128)(4,1)S(1)} %fusion.15), kind=kOutput, calls=%fused_computation.3 | convolution fusion | flops 35717120 | bytes 6299664 | tf_op jit(solution)/shard_map/pkc,pkx->pcx/dot_general | solution.py:36
  189.3 0.0 all-to-all-done
  189.3 8.9 %fusion.5 = f32[256,256]{1,0:T(8,128)} fusion(bf16[16,512,256]{2,1,0:T(8,128)(2,1)} %all-to-all-done, bf16[256,16,512]{2,1,0:T(8,128)(2,1)} %convolution_convert_fusion, f32[256]{0:T(256)S(1)} %convert_element_type.21), kind=kOutput, calls=%fused_computation.6 | convolution fusion | flops 1073807360 | bytes 8651776 | tf_op jit(solution)/shard_map/dot_general | solution.py:40
  (3 shorter events, 0.0 us)
Async XLA Ops:
  6.5 168.4 %all-gather.2.cloned.1.call-start = ((), (), s32[]{:S(2)}) async-start(), calls=%async_computation.1 | async-start | bytes 2162688 | tf_op jit(solution)/shard_map/all_gather | solution.py:32
  10.6 12.2 %copy-start = (s32[16,16]{1,0:T(8,128)S(1)}, s32[16,16]{1,0:T(8,128)}, u32[]{:S(2)}) copy-start(s32[16,16]{1,0:T(8,128)} %param.8) | copy-start | bytes 3076
  10.6 178.7 %all-to-all-start = ((bf16[16,512,256]{2,1,0:T(8,128)(2,1)}), bf16[16,512,256]{2,1,0:T(8,128)(2,1)}, u32[]{:S(2)}, u32[]{:S(2)}) async-start(bf16[16,512,256]{2,1,0:T(8,128)(2,1)} %stack.2), calls=%async_computation | async-start | bytes 8388608 | tf_op jit(solution)/shard_map/all_to_all | solution.py:43
Sparse Core Ops, SparseCore 0:
  10.4 164.4 all-gather.1
